TPU v7x, 256 devices: a whole 4x4x8 slice. The times are simulated.
256 devices in a mesh: seq: 64 (over y, x_hi, z), head: 4 (over x_lo, core).
Axes of the slice: x: 4 (x_hi: 2, x_lo: 2; x = x_hi * 2 + x_lo), y: 4, z: 8, core: 2. Of those that a mesh axis runs over, the one named last changes fastest.
Arguments:
- queries: bfloat16 [10240, 2560], P('seq', 'head'), may hold values from -48 to 48
- keys: bfloat16 [10240, 2560], P('seq', 'head'), may hold values from -9.625 to 9.625
- values: bfloat16 [10240, 2560], P('seq', 'head'), may hold values from -6 to 6
- out_weight: bfloat16 [2560, 5120], P('head'), may hold values from -0.125 to 0.125
Outputs:
- mixed: bfloat16 [10240, 5120], P('seq', 'head')
All inputs are finite; a program needn't handle non-finite values.
Results may differ from a plain program's by a relative error of at most 0.015.
Values may be sent and summed in bfloat16 or wider, within the bound.
A program may use at most 192 MiB of HBM per device.

v0:
```python
import math

import jax
import jax.numpy as jnp
from jax import lax
from jax.sharding import PartitionSpec as P

HD = 128


def in_one_piece(arrays, axis, dim, along):
    widths = [a.shape[along] for a in arrays]
    both = jnp.concatenate(arrays, axis=along)
    out = lax.all_gather(both, axis, axis=dim, tiled=True)
    return tuple(jnp.split(out, [sum(widths[:k]) for k in range(1, len(widths))], axis=along))


def split_up(x, dim, length):
    before, after = (x.shape[:dim], x.shape[dim + 1 :])
    return jnp.moveaxis(x.reshape(*before, length, -1, *after), dim, 0)


def summed_on_arrival(x, axis, dim):
    tiles = split_up(x, dim, lax.axis_size(axis))
    arrived = lax.all_to_all(tiles, axis, split_axis=0, concat_axis=0, tiled=True)
    return arrived.astype(jnp.float32).sum(axis=0)


def block_partial(query_rows, key_block, value_block, scale):
    scores = (
        jnp.einsum("rhd,bhd->hrb", query_rows, key_block, preferred_element_type=jnp.float32)
        * scale
    )
    block_max = jnp.max(scores, axis=-1)
    expo = jnp.exp(scores - block_max[..., None])
    block_total = jnp.sum(expo, axis=-1)
    weights = expo.astype(jnp.bfloat16)
    summed = jnp.einsum("hrb,bhd->rhd", weights, value_block, preferred_element_type=jnp.float32)
    partial_value = (summed / jnp.transpose(block_total)[..., None]).astype(jnp.bfloat16)
    block_log = jnp.transpose(block_max + jnp.log(block_total))
    return (partial_value, block_log)


def group_size(count):
    return max([divisor for divisor in range(1, 9) if count % divisor == 0])


def on_device(queries, keys, values, out_weight):
    rows = queries.shape[0]
    width = queries.shape[1]
    heads = width // HD
    scale = 1.0 / math.sqrt(HD)
    query_local = queries.reshape(rows, heads, HD)
    start_state = (
        jnp.full((rows, heads), -1e30, jnp.float32),
        jnp.zeros((rows, heads, HD), jnp.float32),
    )
    pieces = in_one_piece((keys, values), "seq", 0, 1)
    count = pieces[0].shape[0] // rows
    group = group_size(count)
    key_groups = pieces[0].reshape(count // group, group, rows, heads, HD)
    value_groups = pieces[1].reshape(count // group, group, rows, heads, HD)

    def one_block(key_block, value_block):
        return block_partial(query_local, key_block, value_block, scale)

    def step_group(state, blocks_in):
        partial_value, block_log = jax.vmap(one_block)(blocks_in[0], blocks_in[1])
        run_log, accum = state
        highest = jnp.maximum(run_log, jnp.max(block_log, axis=0))
        new_log = highest + jnp.log(
            jnp.exp(run_log - highest) + jnp.sum(jnp.exp(block_log - highest), axis=0)
        )
        accum = accum * jnp.exp(run_log - new_log)[..., None]
        accum = accum + jnp.sum(partial_value * jnp.exp(block_log - new_log)[..., None], axis=0)
        return ((new_log, accum), None)

    final_state, unused = lax.scan(step_group, start_state, (key_groups, value_groups))
    attended = final_state[1]
    attended_rows = attended.astype(jnp.bfloat16).reshape(rows, width)
    term = jnp.dot(attended_rows, out_weight, preferred_element_type=jnp.float32)
    return summed_on_arrival(term.astype(jnp.bfloat16), "head", 1).astype(jnp.bfloat16)


def solution(mesh):
    placed = (P("seq", "head"), P("seq", "head"), P("seq", "head"), P("head", None))
    return jax.shard_map(
        on_device, mesh=mesh, in_specs=placed, out_specs=P("seq", "head"), check_vma=False
    )
```

profile of v0, /device:TPU:1, one launch (start us, length us, event | category | flops | bytes accessed | tf_op | source)
XLA Modules:
  0.0 528.0 jit_solution(15998233867588102339)
XLA Ops:
  9.2 287.6 %all-gather.2.cloned.1.call-done = bf16[10240,1280]{1,0:T(8,128)(2,1)} async-done(((bf16[160,1280]{1,0:T(8,128)(2,1)}), bf16[10240,1280]{1,0:T(8,128)(2,1)}) %all-gather.2.cloned.1.call-update) | async-done | bytes 26214416 | tf_op jit(solution)/shard_map/all_gather | solution.py:14
  296.8 19.9 %fusion.22 = (bf16[10240,640]{1,0:T(8,128)(2,1)}, bf16[10240,640]{1,0:T(8,128)(2,1)}) fusion(bf16[10240,1280]{1,0:T(8,128)(2,1)} %all-gather.2.cloned.1.call-done), kind=kLoop, calls=%fused_computation.34 | loop fusion | bytes 52428800 | tf_op jit(solution)/shard_map/split | solution.py:15
  316.7 28.9 %reshape.21 = bf16[8,8,160,5,128]{4,3,2,1,0:T(8,128)(2,1)} reshape(bf16[10240,640]{1,0:T(8,128)(2,1)} %get-tuple-element.90) | data formatting | bytes 26214400 | tf_op jit(solution)/shard_map/reshape | solution.py:61
  345.6 15.4 %copy.19 = bf16[8,8,160,5,128]{4,2,1,3,0:T(8,128)(2,1)} copy(bf16[8,8,160,5,128]{4,3,2,1,0:T(8,128)(2,1)} %reshape.21) | data formatting | bytes 26214400
  361.0 28.9 %reshape.23 = bf16[8,8,160,5,128]{4,3,2,1,0:T(8,128)(2,1)} reshape(bf16[10240,640]{1,0:T(8,128)(2,1)} %get-tuple-element.89) | data formatting | bytes 26214400 | tf_op jit(solution)/shard_map/reshape | solution.py:62
  389.9 15.4 %copy.21 = bf16[8,8,160,5,128]{4,2,3,1,0:T(8,128)(2,1)} copy(bf16[8,8,160,5,128]{4,3,2,1,0:T(8,128)(2,1)} %reshape.23) | data formatting | bytes 26214400
  405.3 86.5 %while.13 = (s32[]{:T(128)}, f32[160,5]{0,1:T(8,128)S(1)}, f32[160,5,128]{2,0,1:T(8,128)}, bf16[8,8,160,5,128]{4,2,1,3,0:T(8,128)(2,1)}, bf16[160,5,128]{2,0,1:T...) while((s32[]{:T(128)}, f32[160,5]{0,1:T(8,128)S(1)}, ...), condition=%wide.region_6.7_spmd.clone, body=%wide.region_0.6_spmd.clone.sunk | while | flops 534769600 | bytes 17860320 | solution.py:78
  405.3 2.5 multiply_reduce_fusion.4
  409.7 4.6 multiply_reduce_fusion.5
  415.3 2.5 multiply_reduce_fusion.4
  419.7 4.6 multiply_reduce_fusion.5
  424.3 1.9 fusion.34
  426.2 2.5 multiply_reduce_fusion.4
  430.6 4.6 multiply_reduce_fusion.5
  435.2 1.9 fusion.34
  437.2 2.5 multiply_reduce_fusion.4
  441.6 4.6 multiply_reduce_fusion.5
  446.2 1.9 fusion.34
  448.1 2.5 multiply_reduce_fusion.4
  452.5 4.6 multiply_reduce_fusion.5
  457.1 1.9 fusion.34
  459.0 2.5 multiply_reduce_fusion.4
  463.4 4.6 multiply_reduce_fusion.5
  468.0 1.9 fusion.34
  470.0 2.5 multiply_reduce_fusion.4
  474.4 4.6 multiply_reduce_fusion.5
  479.0 1.9 fusion.34
  480.9 2.5 multiply_reduce_fusion.4
  485.3 4.6 multiply_reduce_fusion.5
  489.9 1.9 fusion.34
  491.9 4.5 convolution_convert_fusion
  496.5 23.6 %all_to_all.5 = bf16[4,160,1280]{2,1,0:T(8,128)(2,1)S(1)} all-to-all(bf16[4,160,1280]{2,1,0:T(8,128)(2,1)S(1)} %bitcast.97), channel_id=1, replica_groups=mesh['seq'=64,'head'=4] {'head'}, dimensions={0} | all-to-all | bytes 3276800 | tf_op jit(solution)/shard_map/all_to_all | solution.py:25
  (77 shorter events, 19.6 us)
Async XLA Ops:
  6.5 1.9 copy-start
  6.5 290.2 %all-gather.2.cloned.1.call-start = ((), (), s32[]{:S(2)}) async-start(), calls=%async_computation.1 | async-start | bytes 26624000 | tf_op jit(solution)/shard_map/all_gather | solution.py:14
  491.9 29.3 %copy-start.1 = (bf16[160,640]{1,0:T(8,128)(2,1)S(1)}, bf16[160,640]{1,0:T(8,128)(2,1)}, u32[]{:S(2)}) copy-start(bf16[160,640]{1,0:T(8,128)(2,1)} %param.6) | copy-start | bytes 614404
Sparse Core Ops, SparseCore 0:
  10.9 285.8 all-gather.1
where the time goes:
time: 530 us; the launch traced here: 528 us
  waiting for transfers between devices  288 us (54%)
  local copies, waits for them, and re-layouts  110 us (21%)
  matrix products  61 us (12%)
  other arithmetic  32 us (6%)
  blocking collectives  23.6 us (4%)
  between operations  13.4 us (3%)
    all_gather x1, waiting for transfers between devices, in_one_piece(): out = lax.all_gather(both, axis, axis=dim, tiled=True)  288 us
    dot_general x8, matrix products, block_partial(): jnp.einsum('hrb,bhd->rhd', weights, value_block, preferred_element_type=j...  36.7 us
    unnamed x7, local copies, waits for them, and re-layouts  31.5 us
    reshape x1, local copies, waits for them, and re-layouts, on_device(): key_groups = pieces[0].reshape(count // group, group, rows, heads, HD)  28.9 us
    reshape x1, local copies, waits for them, and re-layouts, on_device(): value_groups = pieces[1].reshape(count // group, group, rows, heads, HD)  28.9 us
    all_to_all x1, blocking collectives, summed_on_arrival(): lax.all_to_all(tiles, axis, split_axis=0, concat_axis=0, tiled=True)  23.6 us
    split x1, local copies, waits for them, and re-layouts, in_one_piece(): jnp.split(out, [sum(widths[:k]) for k in range(1, len(widths))], axis=along)  19.9 us
    dot_general x8, matrix products, block_partial(): jnp.einsum('rhd,bhd->hrb', query_rows, key_block, preferred_element_type=...  19.8 us
  transfers between devices with their start and end apart: 1, of which 1 were waited for; matrix products, arithmetic and copies ran while one was open for 0% of the time, Pallas kernels for 0%

commit v1 on v0

v1 whole, which is shorter than its diff:
```python
import functools
import math

import jax
import jax.numpy as jnp
from jax import lax
from jax.experimental import pallas as pl
from jax.experimental.pallas import tpu as pltpu
from jax.sharding import PartitionSpec as P

HD = 128
NY, NX, NZ, NXL, NC = 4, 2, 8, 2, 2
PARTS = 2
LOG2E = math.log2(math.e)


def position(slot):
    return (slot + 5) % NZ


class Copies:
    def __init__(self, send_sem, recv_sem):
        self.send_sem, self.recv_sem, self.made = send_sem, recv_sem, []

    def start(self, src, dst, device):
        n = len(self.made)
        copy = pltpu.make_async_remote_copy(
            src_ref=src,
            dst_ref=dst,
            send_sem=self.send_sem.at[n],
            recv_sem=self.recv_sem.at[n],
            device_id=device,
            device_id_type=pl.DeviceIdType.MESH,
        )
        copy.start()
        self.made.append(copy)
        return copy


def kernel(
    q_in, k_in, v_in, w_in, out_ref,
    q_all, k_all, v_all, w_all, acc, stat, part, part_stat, got, got_stat,
    term, core_got, far_got, mine, send_sem, recv_sem, local_sem,
):
    tok, width = q_in.shape
    heads = width // HD
    half = tok // PARTS
    cols = w_in.shape[1] // (NXL * NC)
    scale = LOG2E / math.sqrt(HD)
    copies = Copies(send_sem, recv_sem)

    seq, head = lax.axis_index("seq"), lax.axis_index("head")
    y, xh, z = seq // (NX * NZ), (seq // NZ) % NX, seq % NZ
    xl, core = head // NC, head % NC

    def at(y_, xh_, z_):
        return (y_ * (NX * NZ) + xh_ * NZ + z_, head)

    z_up, z_down = at(y, xh, (z + 1) % NZ), at(y, xh, (z + NZ - 1) % NZ)
    y_up, y_down = at((y + 1) % NY, xh, z), at((y + NY - 1) % NY, xh, z)
    x_far = at(y, 1 - xh, z)
    other_core = (seq, xl * NC + 1 - core)
    other_chip = (seq, (1 - xl) * NC + core)

    def q_rows(slot):
        return q_all.at[pl.ds(position(slot) * tok, tok), :]

    def rows(ref, far, place):
        return ref.at[far, pl.ds(place * tok, tok), :]

    own = [
        pltpu.make_async_copy(q_in, q_rows(0), local_sem.at[0]),
        pltpu.make_async_copy(k_in, rows(k_all, 0, 0), local_sem.at[1]),
        pltpu.make_async_copy(v_in, rows(v_all, 0, 0), local_sem.at[2]),
    ]
    weights = pltpu.make_async_copy(w_in, w_all, local_sem.at[3])
    for copy in own:
        copy.start()
    weights.start()

    partners = (z_up, z_down, y_up, y_down, x_far, other_core, other_chip)
    barrier = pltpu.get_barrier_semaphore()
    for partner in partners:
        pl.semaphore_signal(
            barrier, inc=1, device_id=partner, device_id_type=pl.DeviceIdType.MESH
        )
    stat[...] = jnp.zeros_like(stat)
    part_stat[...] = jnp.zeros_like(part_stat)
    pl.semaphore_wait(barrier, len(partners))

    up = copies.start(q_in, q_rows(7), z_up)
    down = copies.start(q_in, q_rows(1), z_down)
    k_up = copies.start(k_in, rows(k_all, 0, 3), y_up)
    v_down = copies.start(v_in, rows(v_all, 0, 1), y_down)
    v_up = copies.start(v_in, rows(v_all, 0, 3), y_up)
    k_down = copies.start(k_in, rows(k_all, 0, 1), y_down)
    k_far = copies.start(k_in, rows(k_all, 1, 0), x_far)
    v_far = copies.start(v_in, rows(v_all, 1, 0), x_far)

    up.wait_recv()
    up = copies.start(q_rows(7), q_rows(6), z_up)
    down.wait_recv()
    down = copies.start(q_rows(1), q_rows(2), z_down)
    k_up.wait_recv()
    k_fwd = copies.start(rows(k_all, 0, 3), rows(k_all, 0, 2), y_up)
    v_down.wait_recv()
    v_fwd = copies.start(rows(v_all, 0, 1), rows(v_all, 0, 2), y_down)
    up.wait_recv()
    up = copies.start(q_rows(6), q_rows(5), z_up)
    down.wait_recv()
    down = copies.start(q_rows(2), q_rows(3), z_down)
    k_far.wait_recv()
    k_up2 = copies.start(rows(k_all, 1, 0), rows(k_all, 1, 3), y_up)
    k_down2 = copies.start(rows(k_all, 1, 0), rows(k_all, 1, 1), y_down)
    v_far.wait_recv()
    v_down2 = copies.start(rows(v_all, 1, 0), rows(v_all, 1, 1), y_down)
    v_up2 = copies.start(rows(v_all, 1, 0), rows(v_all, 1, 3), y_up)
    up.wait_recv()
    up = copies.start(q_rows(5), q_rows(4), z_up)
    for copy in own:
        copy.wait()
    for copy in (v_up, k_down, k_fwd, v_fwd, down):
        copy.wait_recv()

    def attend(tile, far):
        here = slice(tile * 4 * tok, (tile + 1) * 4 * tok)
        for h in range(heads):
            hs = slice(h * HD, (h + 1) * HD)
            s = lax.dot_general(
                k_all[far, :, hs],
                q_all[here, hs],
                (((1,), (1,)), ((), ())),
                preferred_element_type=jnp.float32,
            )
            top = jnp.max(s, axis=0, keepdims=True) * scale
            if far:
                before = stat[h : h + 1, here]
                top = jnp.maximum(top, before)
            expo = jnp.exp2(s * scale - top)
            total = jnp.sum(expo, axis=0, keepdims=True)
            o = lax.dot_general(
                v_all[far, :, hs],
                expo.astype(jnp.bfloat16),
                (((0,), (0,)), ((), ())),
                preferred_element_type=jnp.float32,
            )
            if far:
                kept = jnp.exp2(before - top)
                total += kept * stat[8 + h : 9 + h, here]
                o += kept * acc[hs, here]
                part[here, hs] = jnp.transpose(o).astype(jnp.bfloat16)
            else:
                acc[hs, here] = o
            stat[h : h + 1, here] = top
            stat[8 + h : 9 + h, here] = total
        if far:
            both = stat[:, here]
            for n in range(4):
                for r in range(PARTS):
                    a = n * tok + r * half
                    part_stat[4 * tile + n, r, :, :half] = both[:, a : a + half]

    def part_rows(slot, r):
        return pl.ds(position(slot) * tok + r * half, half)

    def send_part(n, slot, r, device):
        o = copies.start(part.at[part_rows(slot, r), :], got.at[n, r], device)
        s = copies.start(part_stat.at[position(slot), r], got_stat.at[n, r], device)
        return (o, s)

    def merged(slot, r, arrivals, last):
        stats = [part_stat[position(slot), r]] + [got_stat[n, r] for n in arrivals]
        tops = [s[:8] for s in stats]
        top = functools.reduce(jnp.maximum, tops)
        shares = [jnp.exp2(t - top) for t in tops]
        total = sum(a * s[8:] for a, s in zip(shares, stats))
        if last:
            total = jnp.where(total == 0.0, 1.0, total)
            shares = [a / total for a in shares]
        blank = jnp.zeros((HD - 8 * len(shares), HD), jnp.float32)
        across = jnp.transpose(jnp.concatenate([*shares, blank], axis=0))
        values = [part[part_rows(slot, r), :]] + [got[n, r] for n in arrivals]
        outs = []
        for h in range(heads):
            hs = slice(h * HD, (h + 1) * HD)
            outs.append(
                sum(
                    v[:, hs].astype(jnp.float32) * across[:half, 8 * i + h : 8 * i + h + 1]
                    for i, v in enumerate(values)
                )
            )
        return jnp.concatenate(outs, axis=1).astype(jnp.bfloat16), top, total

    def pass_on(n, slot, r, arrival, device):
        o, top, total = merged(slot, r, (arrival,), False)
        part[part_rows(slot, r), :] = o
        part_stat[position(slot), r, :8] = top
        part_stat[position(slot), r, 8:] = total
        return send_part(n, slot, r, device)

    def arrive(pair):
        for copy in pair:
            copy.wait_recv()

    attend(1, 0)
    k_up2.wait_recv()
    k_fwd2 = copies.start(rows(k_all, 1, 3), rows(k_all, 1, 2), y_up)
    v_down2.wait_recv()
    v_fwd2 = copies.start(rows(v_all, 1, 1), rows(v_all, 1, 2), y_down)
    up.wait_recv()
    attend(0, 0)
    for copy in (k_down2, v_up2, k_fwd2, v_fwd2):
        copy.wait_recv()
    attend(0, 1)
    ups = [send_part(0, 4, r, z_up) for r in range(PARTS)]
    downs = [send_part(4, 5, r, z_down) for r in range(PARTS)]
    attend(1, 1)
    for step in (1, 2):
        for r in range(PARTS):
            arrive(ups[r])
            ups[r] = pass_on(step, 4 - step, r, step - 1, z_up)
            arrive(downs[r])
            downs[r] = pass_on(4 + step, 5 + step, r, 3 + step, z_down)
    for r in range(PARTS):
        arrive(ups[r])
        ups[r] = pass_on(3, 1, r, 2, z_up)

    weights.wait()

    def columns(j):
        return w_all[:, pl.ds(pl.multiple_of(j * cols, cols), cols)]

    far_here, far_there = (1 - xl) * NC + core, (1 - xl) * NC + 1 - core
    near_here, near_there = head, xl * NC + 1 - core
    waits = []
    for r in range(PARTS):
        arrive(ups[r])
        arrive(downs[r])
        attended = merged(0, r, (3, 6), True)[0]

        def product(j):
            return jnp.dot(attended, columns(j), preferred_element_type=jnp.float32)

        term[r, 0] = product(far_there).astype(jnp.bfloat16)
        first = copies.start(term.at[r, 0], core_got.at[r, 0], other_core)
        far = product(far_here)
        first.wait_recv()
        term[r, 1] = (far + core_got[r, 0].astype(jnp.float32)).astype(jnp.bfloat16)
        second = copies.start(term.at[r, 1], far_got.at[r], other_chip)
        term[r, 2] = product(near_there).astype(jnp.bfloat16)
        third = copies.start(term.at[r, 2], core_got.at[r, 1], other_core)
        mine[r] = product(near_here)
        waits.append((second, third))
    for r, pair in enumerate(waits):
        arrive(pair)
        out_ref[r * half : (r + 1) * half, :] = (
            mine[r]
            + core_got[r, 1].astype(jnp.float32)
            + far_got[r].astype(jnp.float32)
        ).astype(jnp.bfloat16)
    for copy in copies.made:
        copy.wait_send()


def on_device(queries, keys, values, out_weight):
    tok, width = queries.shape
    depth = out_weight.shape[1]
    cols = depth // (NXL * NC)
    half = tok // PARTS
    bf16, f32 = jnp.bfloat16, jnp.float32
    anywhere = pl.BlockSpec(memory_space=pl.ANY)
    return pl.pallas_call(
        kernel,
        out_shape=jax.ShapeDtypeStruct((tok, cols), bf16),
        in_specs=[anywhere] * 4,
        out_specs=pl.BlockSpec(memory_space=pltpu.VMEM),
        scratch_shapes=[
            pltpu.VMEM((NZ * tok, width), bf16),
            pltpu.VMEM((NX, NY * tok, width), bf16),
            pltpu.VMEM((NX, NY * tok, width), bf16),
            pltpu.VMEM((width, depth), bf16),
            pltpu.VMEM((width, NZ * tok), f32),
            pltpu.VMEM((16, NZ * tok), f32),
            pltpu.VMEM((NZ * tok, width), bf16),
            pltpu.VMEM((NZ, PARTS, 16, HD), f32),
            pltpu.VMEM((NZ - 1, PARTS, half, width), bf16),
            pltpu.VMEM((NZ - 1, PARTS, 16, HD), f32),
            pltpu.VMEM((PARTS, 3, half, cols), bf16),
            pltpu.VMEM((PARTS, 2, half, cols), bf16),
            pltpu.VMEM((PARTS, half, cols), bf16),
            pltpu.VMEM((PARTS, half, cols), f32),
            pltpu.SemaphoreType.DMA((64,)),
            pltpu.SemaphoreType.DMA((64,)),
            pltpu.SemaphoreType.DMA((4,)),
        ],
        compiler_params=pltpu.CompilerParams(
            collective_id=0, has_side_effects=True, vmem_limit_bytes=56 << 20
        ),
    )(queries, keys, values, out_weight)


def solution(mesh):
    placed = (P("seq", "head"), P("seq", "head"), P("seq", "head"), P("head", None))
    return jax.shard_map(
        on_device, mesh=mesh, in_specs=placed, out_specs=P("seq", "head"), check_vma=False
    )
```

time: 530 us -> 77.6 us (0.15)
  waiting for transfers between devices: 288 us -> 0 us
  local copies, waits for them, and re-layouts: 110 us -> 1.78 us
  Pallas kernels: 0 us -> 75.7 us
  matrix products: 61 us -> 0 us
  other arithmetic: 32 us -> 0 us
  blocking collectives: 23.6 us -> 0 us
  between operations: 13.4 us -> 0.01 us
    all_gather x1 -> x0, waiting for transfers between devices: 288 us -> none  [in_one_piece(): out = lax.all_gather(both, axis, axis=dim, tiled=True)]
    pallas_call x0 -> x1, Pallas kernels: none -> 75.7 us  [on_device(): pl.pallas_call(kernel, out_shape=jax.ShapeDtypeStruct((tok, cols), bf16),...]
    dot_general x17 -> x0, matrix products: 61 us -> none  [the longest x8 36.7 us: block_partial(): jnp.einsum('hrb,bhd->rhd', weights, value_block, preferred_element_type=j...]
    reshape x3 -> x0, local copies, waits for them, and re-layouts: 58 us -> none  [the longest x1 28.9 us: on_device(): key_groups = pieces[0].reshape(count // group, group, rows, heads, HD)]
    unnamed x7 -> x1, local copies, waits for them, and re-layouts: 31.5 us -> 1.78 us
    all_to_all x1 -> x0, blocking collectives: 23.6 us -> none  [summed_on_arrival(): lax.all_to_all(tiles, axis, split_axis=0, concat_axis=0, tiled=True)]
    split x1 -> x0, local copies, waits for them, and re-layouts: 19.9 us -> none  [in_one_piece(): jnp.split(out, [sum(widths[:k]) for k in range(1, len(widths))], axis=along)]
    add x8 -> x0, other arithmetic: 14.6 us -> none  [step_group(): accum + jnp.sum(partial_value * jnp.exp(block_log - new_log)[..., None],...]
  transfers between devices with their start and end apart: 1 -> 0, of which waited for: 1 -> 0; matrix products, arithmetic and copies ran while one was open for 0% -> 0% of each run, Pallas kernels for 0% -> 0%
where the time goes in v1:
time: 77.6 us; the launch traced here: 77.4 us
  Pallas kernels  75.7 us (98%)
  local copies, waits for them, and re-layouts  1.78 us (2%)
    pallas_call x1, Pallas kernels, on_device(): pl.pallas_call(kernel, out_shape=jax.ShapeDtypeStruct((tok, cols), bf16),...  75.7 us
    unnamed x1, local copies, waits for them, and re-layouts  1.78 us

profile of v1, /device:TPU:1, one launch (start us, length us, event | category | flops | bytes accessed | tf_op | source)
XLA Modules:
  0.0 77.4 jit_solution(2649194214776712754)
XLA Ops:
  0.0 75.7 %shard_map.46 = bf16[160,1280]{1,0:T(8,128)(2,1)} custom-call(bf16[160,640]{1,0:T(8,128)(2,1)} %q_in.1, bf16[160,640]{1,0:T(8,128)(2,1)} %k_in.1, bf16[160,640]{1,0:T(8,128)(2,1)} %v_in.1, bf16[640,5120]{1,0:T(8,128)(2,1)} %w_in.1), custom_call_target="tpu_custom_call" | custom-call | tf_op jit(solution)/shard_map/pallas_call | solution.py:272
  75.7 1.8 %copy.6 = bf16[160,1280]{1,0:T(8,128)(2,1)} copy(bf16[160,1280]{1,0:T(8,128)(2,1)} %shard_map.46) | data formatting | bytes 819200

commit v2 on v0

v2 whole, which is shorter than its diff:
```python
import functools
import math

import jax
import jax.numpy as jnp
from jax import lax
from jax.experimental import pallas as pl
from jax.experimental.pallas import tpu as pltpu
from jax.sharding import PartitionSpec as P

HD = 128
NY, NX, NZ, NXL, NC = 4, 2, 8, 2, 2
PARTS = 2
A_HEADS = 3
ORDER = (0, 1, 7, 2, 6, 3, 5, 4)
LANES = 128
LOG2E = math.log2(math.e)
F32, BF16 = jnp.float32, jnp.bfloat16


class Copies:
    def __init__(self, send_sem, recv_sem):
        self.send_sem, self.recv_sem, self.made = send_sem, recv_sem, []

    def start(self, src, dst, device):
        n = len(self.made)
        copy = pltpu.make_async_remote_copy(
            src_ref=src,
            dst_ref=dst,
            send_sem=self.send_sem.at[n],
            recv_sem=self.recv_sem.at[n],
            device_id=device,
            device_id_type=pl.DeviceIdType.MESH,
        )
        copy.start()
        self.made.append(copy)
        return copy


def arrive(*given):
    for copy in given:
        copy.wait_recv()


def combine(stats, values, heads, last):
    tops = [s[:8] for s in stats]
    top = functools.reduce(jnp.maximum, tops)
    shares = [jnp.exp2(t - top) for t in tops]
    total = sum(a * s[8:] for a, s in zip(shares, stats))
    if last:
        total = jnp.where(total == 0.0, 1.0, total)
        shares = [a / total for a in shares]
    blank = jnp.zeros((HD - 8 * len(shares), HD), F32)
    across = jnp.transpose(jnp.concatenate([*shares, blank], axis=0))
    rows = values[0].shape[0]
    outs = []
    for h in range(heads):
        hs = slice(h * HD, (h + 1) * HD)
        outs.append(
            sum(
                v[:, hs].astype(F32) * across[:rows, 8 * i + h : 8 * i + h + 1]
                for i, v in enumerate(values)
            )
        )
    return jnp.concatenate(outs, axis=1).astype(BF16), jnp.concatenate([top, total], axis=0)


def kernel(
    q_in, k_in, v_in, w_in, out_ref,
    qa, ka, va, qb, kb, vb, w_all, acc, stat_a,
    part_a, pst_a, got_a, gst_a, part_b, pst_b, got_b, gst_b, got_x, gst_x,
    att, term, far_got, mine, send_sem, recv_sem, local_sem,
):
    half, width = q_in.shape[1:]
    tok = PARTS * half
    heads = width // HD
    a_width = A_HEADS * HD
    cols = w_in.shape[1] // (NXL * NC)
    tile = NZ * half
    scale = LOG2E / math.sqrt(HD)
    copies = Copies(send_sem, recv_sem)
    start = copies.start
    on_a, on_b = pl.ds(0, a_width), pl.ds(a_width, width - a_width)

    seq, head = lax.axis_index("seq"), lax.axis_index("head")
    y, xh, z = seq // (NX * NZ), (seq // NZ) % NX, seq % NZ
    xl, core = head // NC, head % NC

    def at(y_, xh_, z_):
        return (y_ * (NX * NZ) + xh_ * NZ + z_, head)

    z_up, z_down = at(y, xh, (z + 1) % NZ), at(y, xh, (z + NZ - 1) % NZ)
    y_up, y_down = at((y + 1) % NY, xh, z), at((y + NY - 1) % NY, xh, z)
    x_far = at(y, 1 - xh, z)
    other_core = (seq, xl * NC + 1 - core)
    other_chip = (seq, (1 - xl) * NC + core)

    def qa_rows(slot):
        return pl.ds(ORDER.index(slot) * half, half)

    def qa_at(slot):
        return qa.at[:, qa_rows(slot), :]

    def a_at(ref, far, step):
        return ref.at[far, pl.ds(step * tok, tok), :]

    def qb_rows(far, step):
        return pl.ds((far * NY + step) * half, half)

    def qb_at(far, step):
        return qb.at[:, qb_rows(far, step), :]

    def b_at(ref, slot):
        return ref.at[pl.ds(slot * tok, tok), :]

    own = [
        pltpu.make_async_copy(q_in.at[:, :, on_a], qa_at(0), local_sem.at[0]),
        pltpu.make_async_copy(k_in.at[:, on_a], a_at(ka, 0, 0), local_sem.at[1]),
        pltpu.make_async_copy(v_in.at[:, on_a], a_at(va, 0, 0), local_sem.at[2]),
        pltpu.make_async_copy(q_in.at[:, :, on_b], qb_at(0, 0), local_sem.at[3]),
        pltpu.make_async_copy(k_in.at[:, on_b], b_at(kb, 0), local_sem.at[4]),
        pltpu.make_async_copy(v_in.at[:, on_b], b_at(vb, 0), local_sem.at[5]),
    ]
    my_rows = pl.ds(pl.multiple_of(core * width, width), width)

    def w_columns(x, c):
        return w_in.at[:, pl.ds(pl.multiple_of((x * NC + c) * cols, cols), cols)]

    weights = [
        pltpu.make_async_copy(w_columns(x, core), w_all.at[x, my_rows, :], local_sem.at[6 + x])
        for x in range(NXL)
    ]
    for copy in own:
        copy.start()
    for copy in weights:
        copy.start()

    partners = (z_up, z_down, y_up, y_down, x_far, other_core, other_chip)
    barrier = pltpu.get_barrier_semaphore()
    for partner in partners:
        pl.semaphore_signal(
            barrier, inc=1, device_id=partner, device_id_type=pl.DeviceIdType.MESH
        )
    stat_a[...] = jnp.zeros_like(stat_a)
    pst_a[...] = jnp.zeros_like(pst_a)
    pst_b[...] = jnp.zeros_like(pst_b)
    for copy in own:
        copy.wait()
    pl.semaphore_wait(barrier, len(partners))

    def attend(q, k):
        s = lax.dot_general(k, q, (((1,), (1,)), ((), ())), preferred_element_type=F32)
        return s, jnp.max(s, axis=0, keepdims=True) * scale

    def weigh(s, top, v):
        expo = jnp.exp2(s * scale - top)
        o = lax.dot_general(
            v, expo.astype(BF16), (((0,), (0,)), ((), ())), preferred_element_type=F32
        )
        return jnp.sum(expo, axis=0, keepdims=True), o

    def attend_a(r, lo, hi, far):
        for a in range(lo, hi, LANES):
            here = slice(r * tile + a, r * tile + a + LANES)
            for h in range(A_HEADS):
                hs = slice(h * HD, (h + 1) * HD)
                s, top = attend(qa[r, a : a + LANES, hs], ka[far, :, hs])
                if far:
                    before = stat_a[h : h + 1, here]
                    top = jnp.maximum(top, before)
                total, o = weigh(s, top, va[far, :, hs])
                if far:
                    kept = jnp.exp2(before - top)
                    total += kept * stat_a[8 + h : 9 + h, here]
                    o += kept * acc[hs, here]
                    part_a[r, a : a + LANES, hs] = jnp.transpose(o).astype(BF16)
                else:
                    acc[hs, here] = o
                stat_a[h : h + 1, here] = top
                stat_a[8 + h : 9 + h, here] = total
        if far:
            both = stat_a[:, r * tile : (r + 1) * tile]
            for n, slot in enumerate(ORDER):
                pst_a[r, slot, :, :half] = both[:, n * half : (n + 1) * half]

    def attend_b(r, h):
        hs = slice(h * HD, (h + 1) * HD)
        s, top = attend(qb[r, :, hs], kb[:, hs])
        total, o = weigh(s, top, vb[:, hs])
        o = jnp.transpose(o).astype(BF16)
        for n in range(NX * NY):
            here = slice(n * half, (n + 1) * half)
            part_b[r, n // NY, n % NY, :, hs] = o[here, :]
            pst_b[r, n // NY, n % NY, h : h + 1, :half] = top[:, here]
            pst_b[r, n // NY, n % NY, 8 + h : 9 + h, :half] = total[:, here]

    def long_a(r, d):
        return (NZ - d) % NZ if r else d

    def short_a(r, d):
        return d if r else (NZ - d) % NZ

    def long_b(r, d):
        return (NY - d) % NY if r else d

    def send_a(n, r, slot, device):
        return (
            start(part_a.at[r, qa_rows(slot), :], got_a.at[r, n], device),
            start(pst_a.at[r, slot], gst_a.at[r, n], device),
        )

    def send_b(n, r, step, device):
        return (
            start(part_b.at[r, :, step], got_b.at[r, n], device),
            start(pst_b.at[r, :, step], gst_b.at[r, n], device),
        )

    def pass_on_a(n, r, slot, arrival, device):
        o, stat = combine(
            [pst_a[r, slot], gst_a[r, arrival]],
            [part_a[r, qa_rows(slot), :], got_a[r, arrival]],
            A_HEADS,
            False,
        )
        part_a[r, qa_rows(slot), :] = o
        pst_a[r, slot] = stat
        return send_a(n, r, slot, device)

    longs_a, shorts_a, longs_b, shorts_b, across_b = {}, {}, {}, {}, {}

    def ring(r, step):
        far, near = (z_down, z_up) if r else (z_up, z_down)
        if step:
            arrive(*longs_a[r])
            longs_a[r] = pass_on_a(step, r, long_a(r, 4 - step), step - 1, far)
            if step < 3:
                arrive(*shorts_a[r])
                shorts_a[r] = pass_on_a(4 + step, r, short_a(r, 3 - step), 3 + step, near)
        else:
            longs_a[r] = send_a(0, r, long_a(r, 4), far)
            shorts_a[r] = send_a(4, r, short_a(r, 3), near)

    def plane(r, step):
        far, near = (y_down, y_up) if r else (y_up, y_down)
        if step == 0:
            longs_b[r] = send_b(0, r, 2, far)
            shorts_b[r] = send_b(2, r, long_b(r, 3), near)
        elif step == 1:
            arrive(*longs_b[r])
            d = long_b(r, 1)
            for x in range(NX):
                o, stat = combine(
                    [pst_b[r, x, d], gst_b[r, 0, x]],
                    [part_b[r, x, d], got_b[r, 0, x]],
                    heads - A_HEADS,
                    False,
                )
                part_b[r, x, d] = o
                pst_b[r, x, d] = stat
            longs_b[r] = send_b(1, r, d, far)
        else:
            arrive(*longs_b[r], *shorts_b[r])
            o, stat = combine(
                [pst_b[r, 1, 0], gst_b[r, 1, 1], gst_b[r, 2, 1]],
                [part_b[r, 1, 0], got_b[r, 1, 1], got_b[r, 2, 1]],
                heads - A_HEADS,
                False,
            )
            part_b[r, 1, 0] = o
            pst_b[r, 1, 0] = stat
            across_b[r] = (
                start(part_b.at[r, 1, 0], got_x.at[r], x_far),
                start(pst_b.at[r, 1, 0], gst_x.at[r], x_far),
            )

    def attended(r):
        arrive(*longs_a[r], *shorts_a[r], *across_b[r])
        first = combine(
            [pst_a[r, 0], gst_a[r, 3], gst_a[r, 6]],
            [part_a[r, qa_rows(0), :], got_a[r, 3], got_a[r, 6]],
            A_HEADS,
            True,
        )[0]
        second = combine(
            [pst_b[r, 0, 0], gst_b[r, 1, 0], gst_b[r, 2, 0], gst_x[r]],
            [part_b[r, 0, 0], got_b[r, 1, 0], got_b[r, 2, 0], got_x[r]],
            heads - A_HEADS,
            True,
        )[0]
        return jnp.concatenate([first, second], axis=1)

    qa_u = start(qa_at(0), qa_at(7), z_up)
    qa_d = start(qa_at(0), qa_at(1), z_down)
    k_u = start(a_at(ka, 0, 0), a_at(ka, 0, 3), y_up)
    v_d = start(a_at(va, 0, 0), a_at(va, 0, 1), y_down)
    k_x = start(a_at(ka, 0, 0), a_at(ka, 1, 0), x_far)
    v_x = start(a_at(va, 0, 0), a_at(va, 1, 0), x_far)
    v_u = start(a_at(va, 0, 0), a_at(va, 0, 3), y_up)
    k_d = start(a_at(ka, 0, 0), a_at(ka, 0, 1), y_down)
    w_far = [
        start(w_columns(x, 1 - core), w_all.at[x, my_rows, :], other_core) for x in range(NXL)
    ]
    first = qa_u
    first.wait_send()
    kv_u = [start(b_at(ref, 0), b_at(ref, 7), z_up) for ref in (kb, vb)]
    kv_d = [start(b_at(ref, 0), b_at(ref, 1), z_down) for ref in (kb, vb)]

    arrive(qa_u)
    qa_u = start(qa_at(7), qa_at(6), z_up)
    arrive(qa_d)
    qa_d = start(qa_at(1), qa_at(2), z_down)
    arrive(k_u)
    k_f = start(a_at(ka, 0, 3), a_at(ka, 0, 2), y_up)
    arrive(v_d)
    v_f = start(a_at(va, 0, 1), a_at(va, 0, 2), y_down)
    arrive(k_x, v_x)
    far_a = [
        start(a_at(ref, 1, 0), a_at(ref, 1, step), device)
        for ref in (ka, va)
        for step, device in ((3, y_up), (1, y_down))
    ]
    qb_x = start(qb_at(0, 0), qb_at(1, 0), x_far)
    arrive(*kv_u)
    kv_u = [start(b_at(ref, 7), b_at(ref, 6), z_up) for ref in (kb, vb)]
    arrive(*kv_d)
    kv_d = [start(b_at(ref, 1), b_at(ref, 2), z_down) for ref in (kb, vb)]
    arrive(qa_u)
    qa_u = start(qa_at(6), qa_at(5), z_up)
    arrive(qa_d)
    qa_d = start(qa_at(2), qa_at(3), z_down)
    qb_u = start(qb_at(0, 0), qb_at(0, 3), y_up)
    qb_d = start(qb_at(0, 0), qb_at(0, 1), y_down)
    arrive(k_f, v_f)
    far_a += [start(a_at(ref, 0, 2), a_at(ref, 1, 2), x_far) for ref in (ka, va)]
    arrive(qb_x)
    far_b = [
        start(qb_at(1, 0), qb_at(1, step), device) for step, device in ((3, y_up), (1, y_down))
    ]
    arrive(v_u, k_d)

    attend_a(0, 0, 384, 0)
    attend_a(1, 0, 384, 0)
    arrive(*kv_u)
    kv_u = [start(b_at(ref, 6), b_at(ref, 5), z_up) for ref in (kb, vb)]
    arrive(*kv_d)
    kv_d = [start(b_at(ref, 2), b_at(ref, 3), z_down) for ref in (kb, vb)]
    arrive(qa_u)
    qa_u = start(qa.at[0, qa_rows(5), :], qa.at[0, qa_rows(4), :], z_up)
    arrive(qa_d)
    qa_d = start(qa.at[1, qa_rows(3), :], qa.at[1, qa_rows(4), :], z_down)
    attend_a(0, 384, 512, 0)
    attend_a(1, 384, 512, 0)
    arrive(qb_u, qb_d)
    qb_u = start(qb.at[0, qb_rows(0, 3), :], qb.at[0, qb_rows(0, 2), :], y_up)
    qb_d = start(qb.at[1, qb_rows(0, 1), :], qb.at[1, qb_rows(0, 2), :], y_down)
    arrive(qa_u, qa_d)
    attend_a(0, 512, tile, 0)
    attend_a(1, 512, tile, 0)
    arrive(*far_a)
    arrive(*kv_u)
    k_l = start(b_at(kb, 5), b_at(kb, 4), z_up)
    arrive(*kv_d)
    v_l = start(b_at(vb, 3), b_at(vb, 4), z_down)
    attend_a(0, 0, tile, 1)
    ring(0, 0)
    arrive(qb_u, qb_d)
    far_b.append(start(qb_at(0, 2), qb_at(1, 2), x_far))
    attend_a(1, 0, tile, 1)
    ring(1, 0)
    ring(0, 1)
    arrive(k_l, v_l, *far_b)
    attend_b(0, 0)
    ring(1, 1)
    attend_b(0, 1)
    plane(0, 0)
    ring(0, 2)
    attend_b(1, 0)
    attend_b(1, 1)
    plane(1, 0)
    ring(1, 2)
    ring(0, 3)
    plane(0, 1)
    ring(1, 3)
    plane(1, 1)
    plane(0, 2)
    plane(1, 2)

    for copy in weights:
        copy.wait()
    arrive(*w_far)

    def product(r, x):
        return sum(
            jnp.dot(
                att[r, c],
                w_all[x, c * width : (c + 1) * width, :],
                preferred_element_type=F32,
            )
            for c in range(NC)
        )

    swaps, sums = [], []
    for r in range(PARTS):
        att[r, core] = attended(r)
        swaps.append(start(att.at[r, core], att.at[r, core], other_core))
    for r in range(PARTS):
        arrive(swaps[r])
        term[r] = product(r, 1 - xl).astype(BF16)
        sums.append(start(term.at[r], far_got.at[r], other_chip))
    for r in range(PARTS):
        mine[r] = product(r, xl)
    for r in range(PARTS):
        arrive(sums[r])
        out_ref[r * half : (r + 1) * half, :] = (mine[r] + far_got[r].astype(F32)).astype(BF16)
    for copy in copies.made:
        if copy is not first:
            copy.wait_send()


def on_device(queries, keys, values, out_weight):
    tok, width = queries.shape
    depth = out_weight.shape[1]
    cols = depth // (NXL * NC)
    half = tok // PARTS
    a_width = A_HEADS * HD
    b_width = width - a_width
    anywhere = pl.BlockSpec(memory_space=pl.ANY)
    return pl.pallas_call(
        kernel,
        out_shape=jax.ShapeDtypeStruct((tok, cols), BF16),
        in_specs=[anywhere] * 4,
        out_specs=pl.BlockSpec(memory_space=pltpu.VMEM),
        scratch_shapes=[
            pltpu.VMEM((PARTS, NZ * half, a_width), BF16),
            pltpu.VMEM((NX, NY * tok, a_width), BF16),
            pltpu.VMEM((NX, NY * tok, a_width), BF16),
            pltpu.VMEM((PARTS, NX * NY * half, b_width), BF16),
            pltpu.VMEM((NZ * tok, b_width), BF16),
            pltpu.VMEM((NZ * tok, b_width), BF16),
            pltpu.VMEM((NXL, NC * width, cols), BF16),
            pltpu.VMEM((a_width, NZ * tok), F32),
            pltpu.VMEM((16, NZ * tok), F32),
            pltpu.VMEM((PARTS, NZ * half, a_width), BF16),
            pltpu.VMEM((PARTS, NZ, 16, HD), F32),
            pltpu.VMEM((PARTS, NZ - 1, half, a_width), BF16),
            pltpu.VMEM((PARTS, NZ - 1, 16, HD), F32),
            pltpu.VMEM((PARTS, NX, NY, half, b_width), BF16),
            pltpu.VMEM((PARTS, NX, NY, 16, HD), F32),
            pltpu.VMEM((PARTS, 3, NX, half, b_width), BF16),
            pltpu.VMEM((PARTS, 3, NX, 16, HD), F32),
            pltpu.VMEM((PARTS, half, b_width), BF16),
            pltpu.VMEM((PARTS, 16, HD), F32),
            pltpu.VMEM((PARTS, NC, half, width), BF16),
            pltpu.VMEM((PARTS, half, cols), BF16),
            pltpu.VMEM((PARTS, half, cols), BF16),
            pltpu.VMEM((PARTS, half, cols), F32),
            pltpu.SemaphoreType.DMA((96,)),
            pltpu.SemaphoreType.DMA((96,)),
            pltpu.SemaphoreType.DMA((8,)),
        ],
        compiler_params=pltpu.CompilerParams(
            collective_id=0, has_side_effects=True, vmem_limit_bytes=56 << 20
        ),
    )(queries.reshape(PARTS, half, width), keys, values, out_weight)


def solution(mesh):
    placed = (P("seq", "head"), P("seq", "head"), P("seq", "head"), P("head", None))
    return jax.shard_map(
        on_device, mesh=mesh, in_specs=placed, out_specs=P("seq", "head"), check_vma=False
    )
```

time: 530 us -> 73.6 us (0.14)
  waiting for transfers between devices: 288 us -> 0 us
  local copies, waits for them, and re-layouts: 110 us -> 1.78 us
  Pallas kernels: 0 us -> 70.6 us
  matrix products: 61 us -> 0 us
  other arithmetic: 32 us -> 0 us
  blocking collectives: 23.6 us -> 0 us
  between operations: 13.4 us -> 0.01 us
    all_gather x1 -> x0, waiting for transfers between devices: 288 us -> none  [in_one_piece(): out = lax.all_gather(both, axis, axis=dim, tiled=True)]
    pallas_call x0 -> x1, Pallas kernels: none -> 70.6 us  [on_device(): pl.pallas_call(kernel, out_shape=jax.ShapeDtypeStruct((tok, cols), BF16),...]
    dot_general x17 -> x0, matrix products: 61 us -> none  [the longest x8 36.7 us: block_partial(): jnp.einsum('hrb,bhd->rhd', weights, value_block, preferred_element_type=j...]
    reshape x3 -> x0, local copies, waits for them, and re-layouts: 58 us -> none  [the longest x1 28.9 us: on_device(): key_groups = pieces[0].reshape(count // group, group, rows, heads, HD)]
    unnamed x7 -> x1, local copies, waits for them, and re-layouts: 31.5 us -> 1.78 us
    all_to_all x1 -> x0, blocking collectives: 23.6 us -> none  [summed_on_arrival(): lax.all_to_all(tiles, axis, split_axis=0, concat_axis=0, tiled=True)]
    split x1 -> x0, local copies, waits for them, and re-layouts: 19.9 us -> none  [in_one_piece(): jnp.split(out, [sum(widths[:k]) for k in range(1, len(widths))], axis=along)]
    add x8 -> x0, other arithmetic: 14.6 us -> none  [step_group(): accum + jnp.sum(partial_value * jnp.exp(block_log - new_log)[..., None],...]
  transfers between devices with their start and end apart: 1 -> 0, of which waited for: 1 -> 0; matrix products, arithmetic and copies ran while one was open for 0% -> 0% of each run, Pallas kernels for 0% -> 0%
where the time goes in v2:
time: 73.6 us; the launch traced here: 72.4 us
  Pallas kernels  70.6 us (96%)
  local copies, waits for them, and re-layouts  1.78 us (2%)
    pallas_call x1, Pallas kernels, on_device(): pl.pallas_call(kernel, out_shape=jax.ShapeDtypeStruct((tok, cols), BF16),...  70.6 us
    unnamed x1, local copies, waits for them, and re-layouts  1.78 us

profile of v2, /device:TPU:1, one launch (start us, length us, event | category | flops | bytes accessed | tf_op | source)
XLA Modules:
  0.0 72.4 jit_solution(10536527997542594611)
XLA Ops:
  0.0 70.6 %shard_map.46 = bf16[160,1280]{1,0:T(8,128)(2,1)} custom-call(bf16[2,80,640]{2,1,0:T(8,128)(2,1)} %bitcast.1, bf16[160,640]{1,0:T(8,128)(2,1)} %k_in.1, bf16[160,640]{1,0:T(8,128)(2,1)} %v_in.1, bf16[640,5120]{1,0:T(8,128)(2,1)} %w_in.1), custom_call_target="tpu_custom_call" | custom-call | tf_op jit(solution)/shard_map/pallas_call | solution.py:428
  70.6 1.8 %copy.6 = bf16[160,1280]{1,0:T(8,128)(2,1)} copy(bf16[160,1280]{1,0:T(8,128)(2,1)} %shard_map.46) | data formatting | bytes 819200

commit v3 on v2

--- a/solution.py
+++ b/solution.py
@@ -68,7 +68,7 @@
 def kernel(
     q_in, k_in, v_in, w_in, out_ref,
     qa, ka, va, qb, kb, vb, w_all, acc, stat_a,
-    part_a, pst_a, got_a, gst_a, part_b, pst_b, got_b, gst_b, got_x, gst_x,
+    part_a, pst_a, got_a, gst_a, part_b, pst_b, got_b, gst_b,
     att, term, far_got, mine, send_sem, recv_sem, local_sem,
 ):
     half, width = q_in.shape[1:]
@@ -135,7 +135,13 @@
     for copy in weights:
         copy.start()
 
-    partners = (z_up, z_down, y_up, y_down, x_far, other_core, other_chip)
+    partners = [z_up, z_down, other_core, other_chip]
+    partners += [
+        at((y + step) % NY, 1 - xh if x else xh, z)
+        for x in range(NX)
+        for step in range(NY)
+        if x or step
+    ]
     barrier = pltpu.get_barrier_semaphore()
     for partner in partners:
         pl.semaphore_signal(
@@ -190,29 +196,20 @@
         o = jnp.transpose(o).astype(BF16)
         for n in range(NX * NY):
             here = slice(n * half, (n + 1) * half)
-            part_b[r, n // NY, n % NY, :, hs] = o[here, :]
-            pst_b[r, n // NY, n % NY, h : h + 1, :half] = top[:, here]
-            pst_b[r, n // NY, n % NY, 8 + h : 9 + h, :half] = total[:, here]
+            part_b[r, n, :, hs] = o[here, :]
+            pst_b[r, n, h : h + 1, :half] = top[:, here]
+            pst_b[r, n, 8 + h : 9 + h, :half] = total[:, here]
 
     def long_a(r, d):
         return (NZ - d) % NZ if r else d
 
     def short_a(r, d):
         return d if r else (NZ - d) % NZ
-
-    def long_b(r, d):
-        return (NY - d) % NY if r else d
 
     def send_a(n, r, slot, device):
         return (
             start(part_a.at[r, qa_rows(slot), :], got_a.at[r, n], device),
             start(pst_a.at[r, slot], gst_a.at[r, n], device),
-        )
-
-    def send_b(n, r, step, device):
-        return (
-            start(part_b.at[r, :, step], got_b.at[r, n], device),
-            start(pst_b.at[r, :, step], gst_b.at[r, n], device),
         )
 
     def pass_on_a(n, r, slot, arrival, device):
@@ -226,7 +223,7 @@
         pst_a[r, slot] = stat
         return send_a(n, r, slot, device)
 
-    longs_a, shorts_a, longs_b, shorts_b, across_b = {}, {}, {}, {}, {}
+    longs_a, shorts_a, spread_b = {}, {}, {}
 
     def ring(r, step):
         far, near = (z_down, z_up) if r else (z_up, z_down)
@@ -240,41 +237,20 @@
             longs_a[r] = send_a(0, r, long_a(r, 4), far)
             shorts_a[r] = send_a(4, r, short_a(r, 3), near)
 
-    def plane(r, step):
-        far, near = (y_down, y_up) if r else (y_up, y_down)
-        if step == 0:
-            longs_b[r] = send_b(0, r, 2, far)
-            shorts_b[r] = send_b(2, r, long_b(r, 3), near)
-        elif step == 1:
-            arrive(*longs_b[r])
-            d = long_b(r, 1)
-            for x in range(NX):
-                o, stat = combine(
-                    [pst_b[r, x, d], gst_b[r, 0, x]],
-                    [part_b[r, x, d], got_b[r, 0, x]],
-                    heads - A_HEADS,
-                    False,
-                )
-                part_b[r, x, d] = o
-                pst_b[r, x, d] = stat
-            longs_b[r] = send_b(1, r, d, far)
-        else:
-            arrive(*longs_b[r], *shorts_b[r])
-            o, stat = combine(
-                [pst_b[r, 1, 0], gst_b[r, 1, 1], gst_b[r, 2, 1]],
-                [part_b[r, 1, 0], got_b[r, 1, 1], got_b[r, 2, 1]],
-                heads - A_HEADS,
-                False,
-            )
-            part_b[r, 1, 0] = o
-            pst_b[r, 1, 0] = stat
-            across_b[r] = (
-                start(part_b.at[r, 1, 0], got_x.at[r], x_far),
-                start(pst_b.at[r, 1, 0], gst_x.at[r], x_far),
-            )
+    def plane(r):
+        spread_b[r] = []
+        for step in (2, 1, 3, 0):
+            for x in (1, 0):
+                if x or step:
+                    n = x * NY + step
+                    owner = at((y + step) % NY, 1 - xh if x else xh, z)
+                    spread_b[r] += [
+                        start(part_b.at[r, n], got_b.at[r, n], owner),
+                        start(pst_b.at[r, n], gst_b.at[r, n], owner),
+                    ]
 
     def attended(r):
-        arrive(*longs_a[r], *shorts_a[r], *across_b[r])
+        arrive(*longs_a[r], *shorts_a[r], *spread_b[r])
         first = combine(
             [pst_a[r, 0], gst_a[r, 3], gst_a[r, 6]],
             [part_a[r, qa_rows(0), :], got_a[r, 3], got_a[r, 6]],
@@ -282,15 +258,44 @@
             True,
         )[0]
         second = combine(
-            [pst_b[r, 0, 0], gst_b[r, 1, 0], gst_b[r, 2, 0], gst_x[r]],
-            [part_b[r, 0, 0], got_b[r, 1, 0], got_b[r, 2, 0], got_x[r]],
+            [pst_b[r, 0]] + [gst_b[r, n] for n in range(1, NX * NY)],
+            [part_b[r, 0]] + [got_b[r, n] for n in range(1, NX * NY)],
             heads - A_HEADS,
             True,
         )[0]
         return jnp.concatenate([first, second], axis=1)
 
-    qa_u = start(qa_at(0), qa_at(7), z_up)
-    qa_d = start(qa_at(0), qa_at(1), z_down)
+    def q_piece(r):
+        return lambda slot: qa.at[r, qa_rows(slot), :]
+
+    def kv_piece(ref):
+        return lambda slot: b_at(ref, slot)
+
+    q_streams = [(q_piece(0), True), (q_piece(1), False)]
+    kv_streams = [(kv_piece(kb), True), (kv_piece(vb), False)]
+    moving = {}
+
+    def z_first(streams):
+        for piece, up in streams:
+            moving[piece] = [start(piece(0), piece(7), z_up), start(piece(0), piece(1), z_down)]
+
+    def z_on(streams, d):
+        for piece, up in streams:
+            came_up, came_down = moving[piece]
+            arrive(came_up)
+            nxt = []
+            if d < 3 or up:
+                nxt.append(start(piece(8 - d), piece(7 - d), z_up))
+            arrive(came_down)
+            if d < 3 or not up:
+                nxt.append(start(piece(d), piece(d + 1), z_down))
+            moving[piece] = nxt
+
+    def z_last(streams):
+        for piece, up in streams:
+            arrive(*moving[piece])
+
+    z_first(q_streams)
     k_u = start(a_at(ka, 0, 0), a_at(ka, 0, 3), y_up)
     v_d = start(a_at(va, 0, 0), a_at(va, 0, 1), y_down)
     k_x = start(a_at(ka, 0, 0), a_at(ka, 1, 0), x_far)
@@ -300,38 +305,27 @@
     w_far = [
         start(w_columns(x, 1 - core), w_all.at[x, my_rows, :], other_core) for x in range(NXL)
     ]
-    first = qa_u
-    first.wait_send()
-    kv_u = [start(b_at(ref, 0), b_at(ref, 7), z_up) for ref in (kb, vb)]
-    kv_d = [start(b_at(ref, 0), b_at(ref, 1), z_down) for ref in (kb, vb)]
-
-    arrive(qa_u)
-    qa_u = start(qa_at(7), qa_at(6), z_up)
-    arrive(qa_d)
-    qa_d = start(qa_at(1), qa_at(2), z_down)
+    z_on(q_streams, 1)
+    z_first(kv_streams)
     arrive(k_u)
     k_f = start(a_at(ka, 0, 3), a_at(ka, 0, 2), y_up)
     arrive(v_d)
     v_f = start(a_at(va, 0, 1), a_at(va, 0, 2), y_down)
-    arrive(k_x, v_x)
-    far_a = [
-        start(a_at(ref, 1, 0), a_at(ref, 1, step), device)
-        for ref in (ka, va)
-        for step, device in ((3, y_up), (1, y_down))
-    ]
+    far_a = []
+    for came, ref in ((k_x, ka), (v_x, va)):
+        arrive(came)
+        far_a += [
+            start(a_at(ref, 1, 0), a_at(ref, 1, step), device)
+            for step, device in ((3, y_up), (1, y_down))
+        ]
     qb_x = start(qb_at(0, 0), qb_at(1, 0), x_far)
-    arrive(*kv_u)
-    kv_u = [start(b_at(ref, 7), b_at(ref, 6), z_up) for ref in (kb, vb)]
-    arrive(*kv_d)
-    kv_d = [start(b_at(ref, 1), b_at(ref, 2), z_down) for ref in (kb, vb)]
-    arrive(qa_u)
-    qa_u = start(qa_at(6), qa_at(5), z_up)
-    arrive(qa_d)
-    qa_d = start(qa_at(2), qa_at(3), z_down)
+    z_on(q_streams, 2)
+    z_on(kv_streams, 1)
     qb_u = start(qb_at(0, 0), qb_at(0, 3), y_up)
     qb_d = start(qb_at(0, 0), qb_at(0, 1), y_down)
-    arrive(k_f, v_f)
-    far_a += [start(a_at(ref, 0, 2), a_at(ref, 1, 2), x_far) for ref in (ka, va)]
+    for came, ref in ((k_f, ka), (v_f, va)):
+        arrive(came)
+        far_a.append(start(a_at(ref, 0, 2), a_at(ref, 1, 2), x_far))
     arrive(qb_x)
     far_b = [
         start(qb_at(1, 0), qb_at(1, step), device) for step, device in ((3, y_up), (1, y_down))
@@ -339,51 +333,42 @@
     arrive(v_u, k_d)
 
     attend_a(0, 0, 384, 0)
+    z_on(q_streams, 3)
     attend_a(1, 0, 384, 0)
-    arrive(*kv_u)
-    kv_u = [start(b_at(ref, 6), b_at(ref, 5), z_up) for ref in (kb, vb)]
-    arrive(*kv_d)
-    kv_d = [start(b_at(ref, 2), b_at(ref, 3), z_down) for ref in (kb, vb)]
-    arrive(qa_u)
-    qa_u = start(qa.at[0, qa_rows(5), :], qa.at[0, qa_rows(4), :], z_up)
-    arrive(qa_d)
-    qa_d = start(qa.at[1, qa_rows(3), :], qa.at[1, qa_rows(4), :], z_down)
+    z_on(kv_streams, 2)
     attend_a(0, 384, 512, 0)
     attend_a(1, 384, 512, 0)
-    arrive(qb_u, qb_d)
+    arrive(qb_u)
     qb_u = start(qb.at[0, qb_rows(0, 3), :], qb.at[0, qb_rows(0, 2), :], y_up)
+    arrive(qb_d)
     qb_d = start(qb.at[1, qb_rows(0, 1), :], qb.at[1, qb_rows(0, 2), :], y_down)
-    arrive(qa_u, qa_d)
+    z_last(q_streams)
     attend_a(0, 512, tile, 0)
     attend_a(1, 512, tile, 0)
     arrive(*far_a)
-    arrive(*kv_u)
-    k_l = start(b_at(kb, 5), b_at(kb, 4), z_up)
-    arrive(*kv_d)
-    v_l = start(b_at(vb, 3), b_at(vb, 4), z_down)
     attend_a(0, 0, tile, 1)
     ring(0, 0)
+    z_on(kv_streams, 3)
     arrive(qb_u, qb_d)
     far_b.append(start(qb_at(0, 2), qb_at(1, 2), x_far))
     attend_a(1, 0, tile, 1)
     ring(1, 0)
     ring(0, 1)
-    arrive(k_l, v_l, *far_b)
+    z_last(kv_streams)
+    arrive(*far_b)
+    b_heads = heads - A_HEADS
     attend_b(0, 0)
     ring(1, 1)
-    attend_b(0, 1)
-    plane(0, 0)
+    for h in range(1, b_heads):
+        attend_b(0, h)
+    plane(0)
     ring(0, 2)
-    attend_b(1, 0)
-    attend_b(1, 1)
-    plane(1, 0)
+    for h in range(b_heads):
+        attend_b(1, h)
+    plane(1)
     ring(1, 2)
     ring(0, 3)
-    plane(0, 1)
     ring(1, 3)
-    plane(1, 1)
-    plane(0, 2)
-    plane(1, 2)
 
     for copy in weights:
         copy.wait()
@@ -399,22 +384,21 @@
             for c in range(NC)
         )
 
-    swaps, sums = [], []
+    sums = []
     for r in range(PARTS):
         att[r, core] = attended(r)
-        swaps.append(start(att.at[r, core], att.at[r, core], other_core))
-    for r in range(PARTS):
-        arrive(swaps[r])
+        swap = start(att.at[r, core], att.at[r, core], other_core)
+        if r:
+            mine[r - 1] = product(r - 1, xl)
+        arrive(swap)
         term[r] = product(r, 1 - xl).astype(BF16)
         sums.append(start(term.at[r], far_got.at[r], other_chip))
-    for r in range(PARTS):
-        mine[r] = product(r, xl)
+    mine[r] = product(r, xl)
     for r in range(PARTS):
         arrive(sums[r])
         out_ref[r * half : (r + 1) * half, :] = (mine[r] + far_got[r].astype(F32)).astype(BF16)
     for copy in copies.made:
-        if copy is not first:
-            copy.wait_send()
+        copy.wait_send()
 
 
 def on_device(queries, keys, values, out_weight):
@@ -444,18 +428,16 @@
             pltpu.VMEM((PARTS, NZ, 16, HD), F32),
             pltpu.VMEM((PARTS, NZ - 1, half, a_width), BF16),
             pltpu.VMEM((PARTS, NZ - 1, 16, HD), F32),
-            pltpu.VMEM((PARTS, NX, NY, half, b_width), BF16),
-            pltpu.VMEM((PARTS, NX, NY, 16, HD), F32),
-            pltpu.VMEM((PARTS, 3, NX, half, b_width), BF16),
-            pltpu.VMEM((PARTS, 3, NX, 16, HD), F32),
-            pltpu.VMEM((PARTS, half, b_width), BF16),
-            pltpu.VMEM((PARTS, 16, HD), F32),
+            pltpu.VMEM((PARTS, NX * NY, half, b_width), BF16),
+            pltpu.VMEM((PARTS, NX * NY, 16, HD), F32),
+            pltpu.VMEM((PARTS, NX * NY, half, b_width), BF16),
+            pltpu.VMEM((PARTS, NX * NY, 16, HD), F32),
             pltpu.VMEM((PARTS, NC, half, width), BF16),
             pltpu.VMEM((PARTS, half, cols), BF16),
             pltpu.VMEM((PARTS, half, cols), BF16),
             pltpu.VMEM((PARTS, half, cols), F32),
-            pltpu.SemaphoreType.DMA((96,)),
-            pltpu.SemaphoreType.DMA((96,)),
+            pltpu.SemaphoreType.DMA((128,)),
+            pltpu.SemaphoreType.DMA((128,)),
             pltpu.SemaphoreType.DMA((8,)),
         ],
         compiler_params=pltpu.CompilerParams(

time: 73.6 us -> 69.8 us (0.948); the launches traced: 72.4 us -> 69.7 us
  Pallas kernels: 70.6 us -> 67.9 us
    pallas_call x1, Pallas kernels: 70.6 us -> 67.9 us  [on_device(): pl.pallas_call(kernel, out_shape=jax.ShapeDtypeStruct((tok, cols), BF16),...]
where the time goes in v3:
time: 69.8 us; the launch traced here: 69.7 us
  Pallas kernels  67.9 us (97%)
  local copies, waits for them, and re-layouts  1.78 us (3%)
    pallas_call x1, Pallas kernels, on_device(): pl.pallas_call(kernel, out_shape=jax.ShapeDtypeStruct((tok, cols), BF16),...  67.9 us
    unnamed x1, local copies, waits for them, and re-layouts  1.78 us

profile of v3, /device:TPU:1, one launch (start us, length us, event | category | flops | bytes accessed | tf_op | source)
XLA Modules:
  0.0 69.7 jit_solution(13471634615045520487)
XLA Ops:
  0.0 67.9 %shard_map.46 = bf16[160,1280]{1,0:T(8,128)(2,1)} custom-call(bf16[2,80,640]{2,1,0:T(8,128)(2,1)} %bitcast.1, bf16[160,640]{1,0:T(8,128)(2,1)} %k_in.1, bf16[160,640]{1,0:T(8,128)(2,1)} %v_in.1, bf16[640,5120]{1,0:T(8,128)(2,1)} %w_in.1), custom_call_target="tpu_custom_call" | custom-call | tf_op jit(solution)/shard_map/pallas_call | solution.py:412
  67.9 1.8 %copy.6 = bf16[160,1280]{1,0:T(8,128)(2,1)} copy(bf16[160,1280]{1,0:T(8,128)(2,1)} %shard_map.46) | data formatting | bytes 819200

commit v4 on v3

--- a/solution.py
+++ b/solution.py
@@ -90,6 +90,7 @@
         return (y_ * (NX * NZ) + xh_ * NZ + z_, head)
 
     z_up, z_down = at(y, xh, (z + 1) % NZ), at(y, xh, (z + NZ - 1) % NZ)
+    z_up2, z_down2 = at(y, xh, (z + 2) % NZ), at(y, xh, (z + NZ - 2) % NZ)
     y_up, y_down = at((y + 1) % NY, xh, z), at((y + NY - 1) % NY, xh, z)
     x_far = at(y, 1 - xh, z)
     other_core = (seq, xl * NC + 1 - core)
@@ -135,7 +136,7 @@
     for copy in weights:
         copy.start()
 
-    partners = [z_up, z_down, other_core, other_chip]
+    partners = [z_up, z_down, z_up2, z_down2, other_core, other_chip]
     partners += [
         at((y + step) % NY, 1 - xh if x else xh, z)
         for x in range(NX)
@@ -212,10 +213,10 @@
             start(pst_a.at[r, slot], gst_a.at[r, n], device),
         )
 
-    def pass_on_a(n, r, slot, arrival, device):
+    def pass_on_a(n, r, slot, arrivals, device):
         o, stat = combine(
-            [pst_a[r, slot], gst_a[r, arrival]],
-            [part_a[r, qa_rows(slot), :], got_a[r, arrival]],
+            [pst_a[r, slot]] + [gst_a[r, m] for m in arrivals],
+            [part_a[r, qa_rows(slot), :]] + [got_a[r, m] for m in arrivals],
             A_HEADS,
             False,
         )
@@ -223,19 +224,20 @@
         pst_a[r, slot] = stat
         return send_a(n, r, slot, device)
 
-    longs_a, shorts_a, spread_b = {}, {}, {}
+    longs_a, shorts_a, ends_a, spread_b = {}, {}, {}, {}
 
     def ring(r, step):
         far, near = (z_down, z_up) if r else (z_up, z_down)
-        if step:
+        far2, near2 = (z_down2, z_up2) if r else (z_up2, z_down2)
+        if step == 0:
+            longs_a[r] = send_a(0, r, long_a(r, 4), far2) + send_a(1, r, long_a(r, 3), far)
+            shorts_a[r] = send_a(2, r, short_a(r, 3), near)
+            ends_a[r] = send_a(3, r, long_a(r, 1), far) + send_a(4, r, short_a(r, 1), near)
+        else:
             arrive(*longs_a[r])
-            longs_a[r] = pass_on_a(step, r, long_a(r, 4 - step), step - 1, far)
-            if step < 3:
-                arrive(*shorts_a[r])
-                shorts_a[r] = pass_on_a(4 + step, r, short_a(r, 3 - step), 3 + step, near)
-        else:
-            longs_a[r] = send_a(0, r, long_a(r, 4), far)
-            shorts_a[r] = send_a(4, r, short_a(r, 3), near)
+            longs_a[r] = pass_on_a(5, r, long_a(r, 2), (0, 1), far2)
+            arrive(*shorts_a[r])
+            shorts_a[r] = pass_on_a(6, r, short_a(r, 2), (2,), near2)
 
     def plane(r):
         spread_b[r] = []
@@ -250,10 +252,10 @@
                     ]
 
     def attended(r):
-        arrive(*longs_a[r], *shorts_a[r], *spread_b[r])
+        arrive(*longs_a[r], *shorts_a[r], *ends_a[r], *spread_b[r])
         first = combine(
-            [pst_a[r, 0], gst_a[r, 3], gst_a[r, 6]],
-            [part_a[r, qa_rows(0), :], got_a[r, 3], got_a[r, 6]],
+            [pst_a[r, 0]] + [gst_a[r, n] for n in range(3, 7)],
+            [part_a[r, qa_rows(0), :]] + [got_a[r, n] for n in range(3, 7)],
             A_HEADS,
             True,
         )[0]
@@ -346,29 +348,23 @@
     attend_a(0, 512, tile, 0)
     attend_a(1, 512, tile, 0)
     arrive(*far_a)
-    attend_a(0, 0, tile, 1)
-    ring(0, 0)
     z_on(kv_streams, 3)
     arrive(qb_u, qb_d)
     far_b.append(start(qb_at(0, 2), qb_at(1, 2), x_far))
+    attend_a(0, 0, tile, 1)
+    ring(0, 0)
     attend_a(1, 0, tile, 1)
     ring(1, 0)
-    ring(0, 1)
     z_last(kv_streams)
     arrive(*far_b)
-    b_heads = heads - A_HEADS
-    attend_b(0, 0)
-    ring(1, 1)
-    for h in range(1, b_heads):
+    for h in range(heads - A_HEADS):
         attend_b(0, h)
     plane(0)
-    ring(0, 2)
-    for h in range(b_heads):
+    ring(0, 1)
+    for h in range(heads - A_HEADS):
         attend_b(1, h)
     plane(1)
-    ring(1, 2)
-    ring(0, 3)
-    ring(1, 3)
+    ring(1, 1)
 
     for copy in weights:
         copy.wait()

time: 69.8 us -> 67.3 us (0.964)
  Pallas kernels: 67.9 us -> 65.4 us
    pallas_call x1, Pallas kernels: 67.9 us -> 65.4 us  [on_device(): pl.pallas_call(kernel, out_shape=jax.ShapeDtypeStruct((tok, cols), BF16),...]
where the time goes in v4:
time: 67.3 us; the launch traced here: 67.2 us
  Pallas kernels  65.4 us (97%)
  local copies, waits for them, and re-layouts  1.78 us (3%)
    pallas_call x1, Pallas kernels, on_device(): pl.pallas_call(kernel, out_shape=jax.ShapeDtypeStruct((tok, cols), BF16),...  65.4 us
    unnamed x1, local copies, waits for them, and re-layouts  1.78 us

profile of v4, /device:TPU:1, one launch (start us, length us, event | category | flops | bytes accessed | tf_op | source)
XLA Modules:
  0.0 67.2 jit_solution(16849153467207363666)
XLA Ops:
  0.0 65.4 %shard_map.46 = bf16[160,1280]{1,0:T(8,128)(2,1)} custom-call(bf16[2,80,640]{2,1,0:T(8,128)(2,1)} %bitcast.1, bf16[160,640]{1,0:T(8,128)(2,1)} %k_in.1, bf16[160,640]{1,0:T(8,128)(2,1)} %v_in.1, bf16[640,5120]{1,0:T(8,128)(2,1)} %w_in.1), custom_call_target="tpu_custom_call" | custom-call | tf_op jit(solution)/shard_map/pallas_call | solution.py:408
  65.4 1.8 %copy.6 = bf16[160,1280]{1,0:T(8,128)(2,1)} copy(bf16[160,1280]{1,0:T(8,128)(2,1)} %shard_map.46) | data formatting | bytes 819200

commit v5 on v4

--- a/solution.py
+++ b/solution.py
@@ -123,6 +123,7 @@
         pltpu.make_async_copy(v_in.at[:, on_b], b_at(vb, 0), local_sem.at[5]),
     ]
     my_rows = pl.ds(pl.multiple_of(core * width, width), width)
+    their_rows = pl.ds(pl.multiple_of((1 - core) * width, width), width)
 
     def w_columns(x, c):
         return w_in.at[:, pl.ds(pl.multiple_of((x * NC + c) * cols, cols), cols)]
@@ -381,18 +382,28 @@
         )
 
     sums = []
+    piece = cols // 2
     for r in range(PARTS):
         att[r, core] = attended(r)
         swap = start(att.at[r, core], att.at[r, core], other_core)
-        if r:
-            mine[r - 1] = product(r - 1, xl)
+        share = jnp.dot(att[r, core], w_all[1 - xl, my_rows, :], preferred_element_type=F32)
         arrive(swap)
-        term[r] = product(r, 1 - xl).astype(BF16)
-        sums.append(start(term.at[r], far_got.at[r], other_chip))
-    mine[r] = product(r, xl)
+        for n in range(2):
+            cs = slice(n * piece, (n + 1) * piece)
+            rest = jnp.dot(
+                att[r, 1 - core], w_all[1 - xl, their_rows, cs], preferred_element_type=F32
+            )
+            term[r, n] = (share[:, cs] + rest).astype(BF16)
+            sums.append(start(term.at[r, n], far_got.at[r, n], other_chip))
     for r in range(PARTS):
-        arrive(sums[r])
-        out_ref[r * half : (r + 1) * half, :] = (mine[r] + far_got[r].astype(F32)).astype(BF16)
+        mine[r] = product(r, xl)
+    for r in range(PARTS):
+        for n in range(2):
+            cs = slice(n * piece, (n + 1) * piece)
+            arrive(sums[2 * r + n])
+            out_ref[r * half : (r + 1) * half, cs] = (
+                mine[r, :, cs] + far_got[r, n].astype(F32)
+            ).astype(BF16)
     for copy in copies.made:
         copy.wait_send()
 
@@ -429,8 +440,8 @@
             pltpu.VMEM((PARTS, NX * NY, half, b_width), BF16),
             pltpu.VMEM((PARTS, NX * NY, 16, HD), F32),
             pltpu.VMEM((PARTS, NC, half, width), BF16),
-            pltpu.VMEM((PARTS, half, cols), BF16),
-            pltpu.VMEM((PARTS, half, cols), BF16),
+            pltpu.VMEM((PARTS, 2, half, cols // 2), BF16),
+            pltpu.VMEM((PARTS, 2, half, cols // 2), BF16),
             pltpu.VMEM((PARTS, half, cols), F32),
             pltpu.SemaphoreType.DMA((128,)),
             pltpu.SemaphoreType.DMA((128,)),

time: 67.3 us -> 67.2 us (level)
  no operation moved by 1% of the time
where the time goes in v5:
time: 67.2 us; the launch traced here: 67.1 us
  Pallas kernels  65.3 us (97%)
  local copies, waits for them, and re-layouts  1.78 us (3%)
    pallas_call x1, Pallas kernels, on_device(): pl.pallas_call(kernel, out_shape=jax.ShapeDtypeStruct((tok, cols), BF16),...  65.3 us
    unnamed x1, local copies, waits for them, and re-layouts  1.78 us

profile of v5, /device:TPU:1, one launch (start us, length us, event | category | flops | bytes accessed | tf_op | source)
XLA Modules:
  0.0 67.1 jit_solution(8223533099330312119)
XLA Ops:
  0.0 65.3 %shard_map.46 = bf16[160,1280]{1,0:T(8,128)(2,1)} custom-call(bf16[2,80,640]{2,1,0:T(8,128)(2,1)} %bitcast.1, bf16[160,640]{1,0:T(8,128)(2,1)} %k_in.1, bf16[160,640]{1,0:T(8,128)(2,1)} %v_in.1, bf16[640,5120]{1,0:T(8,128)(2,1)} %w_in.1), custom_call_target="tpu_custom_call" | custom-call | tf_op jit(solution)/shard_map/pallas_call | solution.py:419
  65.3 1.8 %copy.6 = bf16[160,1280]{1,0:T(8,128)(2,1)} copy(bf16[160,1280]{1,0:T(8,128)(2,1)} %shard_map.46) | data formatting | bytes 819200
